TPU v7x, 32 devices: a whole 2x2x4 slice. The times are simulated.
32 devices in a mesh: replica: 4 (over y, core), shard: 8 (over z, x).
Axes of the slice: x: 2, y: 2, z: 4, core: 2. Of those that a mesh axis runs over, the one named last changes fastest.
Arguments:
- tokens: bfloat16 [4, 1024, 3072], P('replica', 'shard'), may hold values from -6 to 6
- weight_slots: bfloat16 [4, 576, 128, 128], P('replica', 'shard'), may hold values from -0.15625 to 0.15625
- block_rows: int32 [96, 12], replicated, may hold values from 0 to 23, as said below
- block_owner: int32 [96, 12], replicated, may hold values from 0 to 7, as said below
- block_slot: int32 [96, 12], replicated, may hold values from 0 to 71, as said below
- grad_act: bfloat16 [4, 1024, 12288], P(None, 'shard', 'replica'), may hold values from -6 to 6
Outputs:
- act_out: bfloat16 [4, 1024, 12288], P(None, 'shard', 'replica')
- grad_tokens: bfloat16 [4, 1024, 3072], P('replica', 'shard')
- grad_slots: float32 [4, 576, 128, 128], P('replica', 'shard')
Inputs may be any that keep to these rules, and one draw needn't show every extreme that they name: `block_rows`: each row holds 12 distinct increasing block rows; within each group of 24 consecutive block columns every block row appears in exactly 12 of them. `block_owner`: within each group of 24 consecutive block columns no owner holds more than 72 blocks, and in every group some owner holds exactly 72. `block_slot`: within each group of 24 consecutive block columns the pairs of owner and slot are distinct.
All inputs are finite; a program needn't handle non-finite values.
Results may differ from a plain program's by a relative error of at most 0.01.
Values may be sent and summed in bfloat16 or wider, within the bound.
A program may use at most 192 MiB of HBM per device.

v0:
```python
import math
import jax
import jax.numpy as jnp
from jax import lax
from jax.sharding import PartitionSpec as P


def gelu_value(hidden):
    return 0.5 * hidden * (1.0 + lax.erf(hidden * 0.7071067811865476))


def gelu_slope(hidden):
    normal_cdf = 0.5 * (1.0 + lax.erf(hidden * 0.7071067811865476))
    return normal_cdf + hidden * jnp.exp(-0.5 * hidden * hidden) * 0.3989422804014327


def local(tokens, weight_slots, block_rows, block_owner, block_slot, grad_act):
    replica_count = lax.axis_size("replica")
    shard_count = lax.axis_size("shard")
    replica_index = lax.axis_index("replica")
    block_size = weight_slots.shape[3]
    capacity = weight_slots.shape[1]
    tok_rows = tokens.shape[1]
    model_width = tokens.shape[2]
    row_blocks = model_width // block_size
    keep_count = block_rows.shape[1]
    slice_cols = grad_act.shape[2] // block_size
    all_rows = replica_count * tok_rows
    own_slots = weight_slots.reshape(capacity, block_size, block_size)
    start_col = replica_index * slice_cols
    rows_here = lax.dynamic_slice_in_dim(block_rows, start_col, slice_cols, 0)
    owner_here = lax.dynamic_slice_in_dim(block_owner, start_col, slice_cols, 0)
    slot_here = lax.dynamic_slice_in_dim(block_slot, start_col, slice_cols, 0)
    place_here = owner_here * capacity + slot_here
    owner_slab = lax.all_gather(own_slots, "shard", axis=0, tiled=True)
    weight_cols = jnp.take(owner_slab, place_here.reshape(-1), axis=0)
    weight_cols = weight_cols.reshape(slice_cols, keep_count * block_size, block_size)
    gathered = lax.all_gather(tokens, "replica", axis=0, tiled=True)
    token_blocks = gathered.reshape(all_rows, row_blocks, block_size)
    cot_cols = jnp.transpose(grad_act.reshape(all_rows, slice_cols, block_size), (1, 0, 2))

    def column_step(grad_rows, inputs):
        rows_col, weight_col, cot_col = inputs
        col_inputs = jnp.take(token_blocks, rows_col, axis=1).reshape(
            all_rows, keep_count * block_size
        )
        hidden = jnp.dot(col_inputs, weight_col, preferred_element_type=jnp.float32)
        act_col = gelu_value(hidden).astype(jnp.bfloat16)
        slope = (cot_col.astype(jnp.float32) * gelu_slope(hidden)).astype(jnp.bfloat16)
        block_grad = lax.dot_general(
            col_inputs, slope, (((0,), (0,)), ((), ())), preferred_element_type=jnp.float32
        )
        back = lax.dot_general(
            slope, weight_col, (((1,), (1,)), ((), ())), preferred_element_type=jnp.float32
        )
        grad_rows = grad_rows.at[:, rows_col].add(back.reshape(all_rows, keep_count, block_size))
        return (grad_rows, (act_col, block_grad))

    start_rows = jnp.zeros((all_rows, row_blocks, block_size), jnp.float32)
    grad_rows, (act_cols, grad_blocks) = lax.scan(
        column_step, start_rows, (rows_here, weight_cols, cot_cols)
    )
    partial_grad = grad_rows.reshape(replica_count, tok_rows, model_width)
    grad_tokens = lax.psum_scatter(
        partial_grad.astype(jnp.bfloat16), "replica", scatter_dimension=0, tiled=True
    )
    grad_scale = 1.0 / math.sqrt(replica_count * shard_count * tok_rows)
    total_blocks = slice_cols * keep_count
    grad_flat = grad_blocks.reshape(total_blocks, block_size, block_size)
    slot_grid = jnp.zeros((shard_count * capacity, block_size, block_size), jnp.float32)
    slot_grid = slot_grid.at[place_here.reshape(-1)].set(grad_flat)
    summed = lax.psum_scatter(
        slot_grid.astype(jnp.bfloat16), "shard", scatter_dimension=0, tiled=True
    ).astype(jnp.float32)
    grad_slots = (summed * grad_scale).reshape(1, capacity, block_size, block_size)
    act_out = jnp.transpose(act_cols, (1, 0, 2)).reshape(
        replica_count, tok_rows, slice_cols * block_size
    )
    return (act_out, grad_tokens, grad_slots)


def solution(mesh):
    return jax.shard_map(
        local,
        mesh=mesh,
        in_specs=(
            P("replica", "shard", None),
            P("replica", "shard", None, None),
            P(),
            P(),
            P(),
            P(None, "shard", "replica"),
        ),
        out_specs=(
            P(None, "shard", "replica"),
            P("replica", "shard", None),
            P("replica", "shard", None, None),
        ),
        check_vma=False,
    )
```

profile of v0, /device:TPU:0, one launch (start us, length us, event | category | flops | bytes accessed | tf_op | source)
XLA Modules:
  0.0 1459.0 jit_solution(657302423886190313)
XLA Ops:
  13.4 27.5 %all-gather.4.cloned.1.call-done = bf16[4,128,3072]{2,1,0:T(8,128)(2,1)} async-done(((bf16[1,128,3072]{2,1,0:T(8,128)(2,1)}), bf16[4,128,3072]{2,1,0:T(8,128)(2,1)}) %all-gather.4.cloned.1.call-update) | async-done | bytes 3145744 | tf_op jit(solution)/shard_map/all_gather | solution.py:38
  46.1 358.8 %all-gather.6.cloned.1.call-done = bf16[1,576,128,128]{3,2,0,1:T(8,128)(2,1)} async-done(((bf16[1,72,128,128]{3,2,0,1:T(8,128)(2,1)}), bf16[1,576,128,128]{3,2,0,1:T(8,128)(2,1)}) %all-gather.6.cloned.1.call-update) | async-done | bytes 18874384 | tf_op jit(solution)/shard_map/all_gather | solution.py:35
  404.9 16.8 %gather_fusion.1 = bf16[288,128,128]{2,1,0:T(8,128)(2,1)} fusion(bf16[576,128,128]{2,1,0:T(8,128)(2,1)} %bitcast.109, s32[1024]{0:T(1024)S(1)} %pad_clamp_fusion.1), kind=kCustom, calls=%fused_computation.1 | custom fusion | bytes 18875520 | tf_op jit(solution)/shard_map/jit(_take)/gather | solution.py:36
  421.7 10.4 bitcast_select_fusion.1
  432.1 3.3 broadcast_in_dim.54
  435.4 577.5 %while.14 = (s32[]{:T(128)}, f32[512,24,128]{2,0,1:T(8,128)}, bf16[24,512,128]{2,1,0:T(8,128)(2,1)}, f32[24,1536,128]{2,1,0:T(8,128)}, s32[24,12]{1,0:T(8,128)},...) while((s32[]{:T(128)}, f32[512,24,128]{2,0,1:T(8,128)}, ...), condition=%wide.region_2.3_spmd, body=%wide.region_0.0_spmd.sunk | while | flops 608109696 | bytes 43393552 | solution.py:60
  448.4 8.1 scatter_fusion
  456.5 2.9 fusion.34
  472.4 8.1 scatter_fusion
  480.5 3.0 fusion.34
  496.5 8.1 scatter_fusion
  504.5 3.0 fusion.34
  520.5 8.1 scatter_fusion
  528.6 2.9 fusion.34
  544.5 8.1 scatter_fusion
  552.6 3.0 fusion.34
  568.5 8.1 scatter_fusion
  576.6 3.0 fusion.34
  592.6 8.1 scatter_fusion
  600.7 3.0 fusion.34
  616.6 8.1 scatter_fusion
  624.7 3.0 fusion.34
  640.7 8.2 scatter_fusion
  648.9 3.0 fusion.34
  664.8 8.1 scatter_fusion
  672.9 3.0 fusion.34
  688.8 8.1 scatter_fusion
  696.9 3.0 fusion.34
  712.9 8.1 scatter_fusion
  721.0 3.0 fusion.34
  736.9 8.2 scatter_fusion
  745.1 3.0 fusion.34
  761.1 8.1 scatter_fusion
  769.2 3.0 fusion.34
  785.1 8.1 scatter_fusion
  793.2 3.0 fusion.34
  809.2 8.2 scatter_fusion
  817.4 3.0 fusion.34
  833.3 8.2 scatter_fusion
  841.5 2.9 fusion.34
  857.4 8.2 scatter_fusion
  865.6 3.0 fusion.34
  881.5 8.1 scatter_fusion
  889.6 3.0 fusion.34
  905.6 8.1 scatter_fusion
  913.6 2.9 fusion.34
  929.6 8.1 scatter_fusion
  937.7 3.0 fusion.34
  953.6 8.1 scatter_fusion
  961.8 3.0 fusion.34
  977.7 8.1 scatter_fusion
  985.8 3.0 fusion.34
  1001.8 8.2 scatter_fusion
  1010.0 2.9 fusion.34
  1012.9 12.6 broadcast_in_dim.61
  1025.5 52.1 %scatter_fusion.1 = f32[576,128,128]{2,1,0:T(8,128)} fusion(f32[576,128,128]{2,1,0:T(8,128)} %broadcast_in_dim.61, s32[288]{0:T(512)S(1)} %copy-done.7, f32[288,128,128]{2,1,0:T(8,128)} %bitcast.106), kind=kCustom, calls=%fused_computation.3 | custom fusion | bytes 56624256 | tf_op jit(solution)/shard_map/scatter | solution.py:71
  1077.7 20.9 %convert_element_type.26 = bf16[576,128,128]{2,1,0:T(8,128)(2,1)} convert(f32[576,128,128]{2,1,0:T(8,128)} %scatter_fusion.1) | non-fusion elementwise | flops 9437184 | bytes 56623104 | tf_op jit(solution)/shard_map/convert_element_type | solution.py:73
  1098.8 3.4 convert_element_type.24
  1104.2 2.8 convert_element_type.25
  1107.1 3.9 copy.38
  1111.0 2.8 reshape.145
  1113.8 298.6 %reduce-scatter.5.cloned.1.call-done = bf16[72,128,128]{2,1,0:T(8,128)(2,1)} async-done(((bf16[576,128,128]{2,1,0:T(8,128)(2,1)}), bf16[72,128,128]{2,1,0:T(8,128)(2,1)}) %reduce-scatter.5.cloned.1.call-update) | async-done | bytes 2359312 | tf_op jit(solution)/shard_map/reduce_scatter | solution.py:72
  1412.4 4.5 multiply_bitcast_fusion
  1416.9 35.6 %reduce-scatter.3.cloned.1.call-done = bf16[1,128,3072]{2,1,0:T(8,128)(2,1)} async-done(((bf16[4,128,3072]{2,1,0:T(8,128)(2,1)}), bf16[1,128,3072]{2,1,0:T(8,128)(2,1)}) %reduce-scatter.3.cloned.1.call-update) | async-done | bytes 786448 | tf_op jit(solution)/shard_map/reduce_scatter | solution.py:64
  (471 shorter events, 323.7 us)
Async XLA Ops:
  7.2 1.6 copy-start
  7.2 2.4 copy-start.8
  7.2 2.4 copy-start.9
  7.2 2.9 copy-start.5
  7.2 33.7 %all-gather.4.cloned.1.call-start = ((), (), s32[]{:S(2)}) async-start(), calls=%async_computation.2 | async-start | bytes 3932160 | tf_op jit(solution)/shard_map/all_gather | solution.py:38
  7.9 397.0 %all-gather.6.cloned.1.call-start = ((), (), s32[]{:S(2)}) async-start(), calls=%async_computation.5 | async-start | bytes 21233664 | tf_op jit(solution)/shard_map/all_gather | solution.py:35
  8.7 1403.7 %reduce-scatter.5.cloned.1.call-start = ((), (), s32[]{:S(2)}) async-start(), calls=%async_computation.4 | async-start | bytes 21233664 | tf_op jit(solution)/shard_map/reduce_scatter | solution.py:72
  13.3 30.3 %copy-start.6 = (s32[288]{0:T(512)}, s32[288]{0:T(512)S(1)}, u32[]{:S(2)}) copy-start(s32[288]{0:T(512)S(1)} %fusion.15) | copy-start | bytes 3460
  443.2 1.7 copy-start.2
  448.4 8.1 copy-start.4
  467.2 1.7 copy-start.2
  472.4 8.1 copy-start.4
  491.2 1.7 copy-start.2
  496.4 8.1 copy-start.4
  515.3 1.7 copy-start.2
  520.5 8.1 copy-start.4
  539.3 1.7 copy-start.2
  542.3 0.7 copy-start.3
  544.5 8.1 copy-start.4
  563.3 1.7 copy-start.2
  568.5 8.1 copy-start.4
  587.4 1.7 copy-start.2
  592.6 8.1 copy-start.4
  611.4 1.7 copy-start.2
  616.6 8.1 copy-start.4
  635.5 1.7 copy-start.2
  640.7 8.2 copy-start.4
  659.6 1.7 copy-start.2
  662.6 0.7 copy-start.3
  664.8 8.1 copy-start.4
  683.6 1.7 copy-start.2
  688.8 8.1 copy-start.4
  707.7 1.7 copy-start.2
  712.9 8.1 copy-start.4
  731.7 1.7 copy-start.2
  736.9 8.2 copy-start.4
  755.9 1.7 copy-start.2
  761.1 8.1 copy-start.4
  779.9 1.7 copy-start.2
  785.1 8.2 copy-start.4
  804.0 1.7 copy-start.2
  809.2 8.2 copy-start.4
  828.1 1.7 copy-start.2
  831.1 0.7 copy-start.3
  833.3 8.2 copy-start.4
  852.2 1.7 copy-start.2
  855.2 0.7 copy-start.3
  857.4 8.2 copy-start.4
  876.3 1.7 copy-start.2
  881.5 8.1 copy-start.4
  900.3 1.7 copy-start.2
  905.6 8.1 copy-start.4
  924.3 1.7 copy-start.2
  929.5 8.1 copy-start.4
  948.4 1.7 copy-start.2
  951.4 0.7 copy-start.3
  953.6 8.2 copy-start.4
  972.5 1.7 copy-start.2
  977.7 8.1 copy-start.4
  996.6 1.7 copy-start.2
  1001.8 8.2 copy-start.4
  1012.9 12.6 copy-start.7
  1098.6 353.9 %reduce-scatter.3.cloned.1.call-start = ((), (), s32[]{:S(2)}) async-start(), calls=%async_computation.3 | async-start | bytes 3932160 | tf_op jit(solution)/shard_map/reduce_scatter | solution.py:64
  1111.0 341.5 %copy-start.1 = (s32[96,12]{0,1:T(8,128)S(1)}, s32[96,12]{0,1:T(8,128)}, u32[]{:S(2)}) copy-start(s32[96,12]{0,1:T(8,128)} %param.10) | copy-start | bytes 13828
  (19 other events, 13.3 us)
Sparse Core Ops, SparseCore 0:
  9.6 31.2 all-gather.3
  42.4 362.4 all-gather.5
  1098.7 313.6 reduce-scatter.4
  1415.4 37.0 reduce-scatter.2
where the time goes:
time: 1470 us; the launch traced here: 1460 us
  waiting for transfers between devices  722 us (49%)
  other arithmetic  308 us (21%)
  local copies, waits for them, and re-layouts  276 us (19%)
  matrix products  137 us (9%)
    all_gather x1, waiting for transfers between devices, local(): owner_slab = lax.all_gather(own_slots, 'shard', axis=0, tiled=True)  359 us
    reduce_scatter x1, waiting for transfers between devices, local(): lax.psum_scatter(slot_grid.astype(jnp.bfloat16), 'shard', scatter_dimensi...  299 us
    scatter-add x24, other arithmetic, column_step(): grad_rows.at[:, rows_col]  195 us
    gather x48, local copies, waits for them, and re-layouts, column_step(): jnp.take(token_blocks, rows_col, axis=1)  82.4 us
    dot_general x24, matrix products, column_step(): lax.dot_general(col_inputs, slope, (((0,), (0,)), ((), ())), preferred_el...  71.1 us
    scatter x1, local copies, waits for them, and re-layouts, local(): slot_grid = slot_grid.at[place_here.reshape(-1)].set(grad_flat)  52.1 us
    select_n x48, other arithmetic, column_step(): jnp.take(token_blocks, rows_col, axis=1)  40.8 us
    select_n x24, local copies, waits for them, and re-layouts, column_step(): jnp.take(token_blocks, rows_col, axis=1)  38.5 us
  transfers between devices with their start and end apart: 4, of which 4 were waited for; matrix products, arithmetic and copies ran while one was open for 2% of the time, Pallas kernels for 0%

commit v1 on v0

--- a/solution.py
+++ b/solution.py
@@ -3,6 +3,28 @@
 import jax.numpy as jnp
 from jax import lax
 from jax.sharding import PartitionSpec as P
+
+
+def in_order(parts, dim):
+    lengths = list(parts.shape[1:])
+    lengths[dim] *= parts.shape[0]
+    return jnp.moveaxis(parts, 0, dim).reshape(lengths)
+
+
+def collect(x, axis, dim):
+    size = lax.axis_size(axis)
+    pairs = [(i, (i + 1) % size) for i in range(size)]
+    back = [(b, a) for a, b in pairs]
+    lower, upper = ([], [])
+    for turn in range(size - 1):
+        if turn % 2 == 0:
+            lower.append(lax.ppermute(lower[-1] if lower else x, axis, pairs))
+        else:
+            upper.append(lax.ppermute(upper[-1] if upper else x, axis, back))
+    blocks = jnp.stack([*lower[::-1], x, *upper])
+    shift = lax.axis_index(axis) - len(lower)
+    blocks = blocks[(jnp.arange(size) - shift) % size]
+    return in_order(blocks, dim)
 
 
 def gelu_value(hidden):
@@ -32,7 +54,7 @@
     owner_here = lax.dynamic_slice_in_dim(block_owner, start_col, slice_cols, 0)
     slot_here = lax.dynamic_slice_in_dim(block_slot, start_col, slice_cols, 0)
     place_here = owner_here * capacity + slot_here
-    owner_slab = lax.all_gather(own_slots, "shard", axis=0, tiled=True)
+    owner_slab = collect(own_slots, "shard", 0)
     weight_cols = jnp.take(owner_slab, place_here.reshape(-1), axis=0)
     weight_cols = weight_cols.reshape(slice_cols, keep_count * block_size, block_size)
     gathered = lax.all_gather(tokens, "replica", axis=0, tiled=True)

time: 1470 us -> 1510 us (1.027)
  waiting for transfers between devices: 722 us -> 568 us
  starting transfers between devices: 0.34 us -> 116 us
  local copies, waits for them, and re-layouts: 276 us -> 329 us
  matrix products: 137 us -> 171 us
    all_gather x1 -> x0, waiting for transfers between devices: 359 us -> none  [local(): owner_slab = lax.all_gather(own_slots, 'shard', axis=0, tiled=True)]
    ppermute x0 -> x7, waiting for transfers between devices: none -> 235 us  [the longest x4 235 us: collect(): lower.append(lax.ppermute(lower[-1] if lower else x, axis, pairs))]
    ppermute x0 -> x7, starting transfers between devices: none -> 116 us  [the longest x3 108 us: collect(): upper.append(lax.ppermute(upper[-1] if upper else x, axis, back))]
    gather x0 -> x16, local copies, waits for them, and re-layouts: none -> 36.9 us
    dot_general x24, matrix products: 30.6 us -> 64.4 us  [column_step(): hidden = jnp.dot(col_inputs, weight_col, preferred_element_type=jnp.float32)]
    all_gather x1, waiting for transfers between devices: 27.5 us -> 0.02 us  [local(): gathered = lax.all_gather(tokens, 'replica', axis=0, tiled=True)]
    unnamed x18 -> x23, local copies, waits for them, and re-layouts: 4.34 us -> 23.7 us
  transfers between devices with their start and end apart: 4 -> 10, of which waited for: 4 -> 6; matrix products, arithmetic and copies ran while one was open for 2% -> 3% of each run, Pallas kernels for 0% -> 0%
where the time goes in v1:
time: 1510 us; the launch traced here: 1500 us
  waiting for transfers between devices  568 us (38%)
  local copies, waits for them, and re-layouts  329 us (22%)
  other arithmetic  306 us (20%)
  matrix products  171 us (11%)
  starting transfers between devices  116 us (8%)
    reduce_scatter x1, waiting for transfers between devices, local(): lax.psum_scatter(slot_grid.astype(jnp.bfloat16), 'shard', scatter_dimensi...  297 us
    ppermute x4, waiting for transfers between devices, collect(): lower.append(lax.ppermute(lower[-1] if lower else x, axis, pairs))  235 us
    scatter-add x24, other arithmetic, column_step(): grad_rows.at[:, rows_col]  192 us
    ppermute x3, starting transfers between devices, collect(): upper.append(lax.ppermute(upper[-1] if upper else x, axis, back))  108 us
    gather x48, local copies, waits for them, and re-layouts, column_step(): jnp.take(token_blocks, rows_col, axis=1)  82.4 us
    dot_general x24, matrix products, column_step(): lax.dot_general(col_inputs, slope, (((0,), (0,)), ((), ())), preferred_el...  71.2 us
    dot_general x24, matrix products, column_step(): hidden = jnp.dot(col_inputs, weight_col, preferred_element_type=jnp.float32)  64.4 us
    scatter x1, local copies, waits for them, and re-layouts, local(): slot_grid = slot_grid.at[place_here.reshape(-1)].set(grad_flat)  52.3 us
  transfers between devices with their start and end apart: 10, of which 6 were waited for; matrix products, arithmetic and copies ran while one was open for 3% of the time, Pallas kernels for 0%

profile of v1, /device:TPU:0, one launch (start us, length us, event | category | flops | bytes accessed | tf_op | source)
XLA Modules:
  0.0 1504.9 jit_solution(11443031497835739245)
XLA Ops:
  7.2 3.0 collective-permute-start
  10.2 54.5 %collective-permute-done = bf16[72,128,128]{2,1,0:T(8,128)(2,1)S(1)} collective-permute-done((bf16[72,128,128]{2,1,0:T(8,128)(2,1)}, bf16[72,128,128]{2,1,0:T(8,128)(2,1)S(1)}, u32[]{:S(2)}, u32[]{:S(2)}) %collective-permute-start) | collective-permute-done | bytes 2359328 | tf_op jit(solution)/shard_map/ppermute | solution.py:21
  64.7 4.7 collective-permute-start.4
  69.5 96.0 %collective-permute-done.1 = bf16[72,128,128]{2,1,0:T(8,128)(2,1)} collective-permute-done((bf16[72,128,128]{2,1,0:T(8,128)(2,1)S(1)}, bf16[72,128,128]{2,1,0:T(8,128)(2,1)}, u32[]{:S(2)}, u32[]{:S(2)}) %collective-permute-start.1) | collective-permute-done | bytes 2359328 | tf_op jit(solution)/shard_map/ppermute | solution.py:21
  168.1 51.5 %collective-permute-start.5 = (bf16[72,128,128]{2,1,0:T(8,128)(2,1)}, bf16[72,128,128]{2,1,0:T(8,128)(2,1)}, u32[]{:S(2)}, u32[]{:S(2)}) collective-permute-start(bf16[72,128,128]{2,1,0:T(8,128)(2,1)} %collective-permute-done.4), channel_id=1, source_target_pairs={{1,0},{2,1},{3,2},{4,3},{5,4},{6,5},{7,6},{0,7},{9,8},{10,9},{11,1... | collective-permute-start | bytes 7077896 | tf_op jit(solution)/shard_map/ppermute | solution.py:23
  219.6 48.7 %collective-permute-done.2 = bf16[72,128,128]{2,1,0:T(8,128)(2,1)} collective-permute-done((bf16[72,128,128]{2,1,0:T(8,128)(2,1)}, bf16[72,128,128]{2,1,0:T(8,128)(2,1)}, u32[]{:S(2)}, u32[]{:S(2)}) %collective-permute-start.2) | collective-permute-done | bytes 2359328 | tf_op jit(solution)/shard_map/ppermute | solution.py:21
  271.9 51.8 %collective-permute-start.6 = (bf16[72,128,128]{2,1,0:T(8,128)(2,1)}, bf16[72,128,128]{2,1,0:T(8,128)(2,1)}, u32[]{:S(2)}, u32[]{:S(2)}) collective-permute-start(bf16[72,128,128]{2,1,0:T(8,128)(2,1)} %collective-permute-done.5), channel_id=1, source_target_pairs={{1,0},{2,1},{3,2},{4,3},{5,4},{6,5},{7,6},{0,7},{9,8},{10,9},{11,1... | collective-permute-start | bytes 7077896 | tf_op jit(solution)/shard_map/ppermute | solution.py:23
  334.9 36.3 %collective-permute-done.3 = bf16[72,128,128]{2,1,0:T(8,128)(2,1)} collective-permute-done((bf16[72,128,128]{2,1,0:T(8,128)(2,1)}, bf16[72,128,128]{2,1,0:T(8,128)(2,1)}, u32[]{:S(2)}, u32[]{:S(2)}) %collective-permute-start.3) | collective-permute-done | bytes 2359328 | tf_op jit(solution)/shard_map/ppermute | solution.py:21
  384.4 6.5 copy-done.4
  390.9 36.9 %while.16 = (s32[]{:T(128)}, bf16[8,72,128,128]{3,2,1,0:T(8,128)(2,1)}, s32[8,1]{0,1:T(1,128)S(1)}, bf16[8,72,128,128]{3,2,1,0:T(8,128)(2,1)}, s32[]{:T(128)}) while((s32[]{:T(128)}, bf16[8,72,128,128]{3,2,1,0:T(8,128)(2,1)}, s32[8,1]{0,1:T(1,128)S(1)}, bf16[8,72,128,128]{3,2,1,0:T(8,128)(2,1)}, s32[]{:T(128)}) %tuple.52), condition=%wide.while_cond, body=%wide.while_body.sunk | while | flops 2 | bytes 4719189 | solution.py:26
  391.5 4.0 dynamic-slice_dynamic-update-slice_fusion.2
  396.1 4.0 dynamic-slice_dynamic-update-slice_fusion.2
  400.7 4.0 dynamic-slice_dynamic-update-slice_fusion.2
  405.3 4.1 dynamic-slice_dynamic-update-slice_fusion.2
  410.0 4.0 dynamic-slice_dynamic-update-slice_fusion.2
  414.5 4.1 dynamic-slice_dynamic-update-slice_fusion.2
  419.2 4.0 dynamic-slice_dynamic-update-slice_fusion.2
  423.8 4.0 dynamic-slice_dynamic-update-slice_fusion.2
  427.8 16.8 %gather_fusion.1 = bf16[288,128,128]{2,1,0:T(8,128)(2,1)} fusion(bf16[576,128,128]{2,1,0:T(8,128)(2,1)} %bitcast.126, s32[1024]{0:T(1024)S(1)} %pad_clamp_fusion.1), kind=kCustom, calls=%fused_computation.1 | custom fusion | bytes 18875520 | tf_op jit(solution)/shard_map/jit(_take)/gather | solution.py:58
  444.6 10.4 bitcast_select_fusion.1
  455.0 3.3 broadcast_in_dim.55
  458.3 601.9 %while.15 = (s32[]{:T(128)}, f32[512,24,128]{2,0,1:T(8,128)}, bf16[24,512,128]{2,1,0:T(8,128)(2,1)}, f32[24,1536,128]{2,1,0:T(8,128)}, s32[24,12]{1,0:T(8,128)},...) while((s32[]{:T(128)}, f32[512,24,128]{2,0,1:T(8,128)}, ...), condition=%wide.region_2.3_spmd, body=%wide.region_0.2_spmd.sunk | while | flops 608109696 | bytes 37102068 | solution.py:82
  472.4 7.9 scatter_fusion
  497.4 8.0 scatter_fusion
  522.5 8.0 scatter_fusion
  530.4 3.0 fusion.35
  547.5 8.0 scatter_fusion
  572.6 7.9 scatter_fusion
  597.6 8.0 scatter_fusion
  605.6 3.0 fusion.35
  622.7 8.0 scatter_fusion
  647.7 8.0 scatter_fusion
  655.7 3.0 fusion.35
  672.8 8.1 scatter_fusion
  697.9 8.0 scatter_fusion
  723.0 7.9 scatter_fusion
  730.9 3.0 fusion.35
  748.0 7.9 scatter_fusion
  755.9 3.0 fusion.35
  773.0 8.1 scatter_fusion
  781.1 3.0 fusion.35
  798.2 8.0 scatter_fusion
  823.2 8.0 scatter_fusion
  848.3 8.1 scatter_fusion
  873.5 8.1 scatter_fusion
  898.6 8.1 scatter_fusion
  923.8 8.0 scatter_fusion
  948.9 8.0 scatter_fusion
  973.9 8.0 scatter_fusion
  981.9 3.0 fusion.35
  999.0 8.0 scatter_fusion
  1007.0 3.0 fusion.35
  1024.1 8.0 scatter_fusion
  1032.1 3.0 fusion.35
  1049.2 8.1 scatter_fusion
  1060.2 12.6 broadcast_in_dim.62
  1072.8 52.3 %scatter_fusion.1 = f32[576,128,128]{2,1,0:T(8,128)} fusion(f32[576,128,128]{2,1,0:T(8,128)} %broadcast_in_dim.62, s32[288]{0:T(512)S(1)} %copy-done.7, f32[288,128,128]{2,1,0:T(8,128)} %bitcast.123), kind=kCustom, calls=%fused_computation.3 | custom fusion | bytes 56624256 | tf_op jit(solution)/shard_map/scatter | solution.py:93
  1125.1 20.9 %convert_element_type.26 = bf16[576,128,128]{2,1,0:T(8,128)(2,1)} convert(f32[576,128,128]{2,1,0:T(8,128)} %scatter_fusion.1) | non-fusion elementwise | flops 9437184 | bytes 56623104 | tf_op jit(solution)/shard_map/convert_element_type | solution.py:95
  1146.1 3.4 convert_element_type.24
  1151.5 3.1 convert_element_type.25
  1154.6 3.9 copy.37
  1161.3 296.8 %reduce-scatter.5.cloned.1.call-done = bf16[72,128,128]{2,1,0:T(8,128)(2,1)} async-done(((bf16[576,128,128]{2,1,0:T(8,128)(2,1)}), bf16[72,128,128]{2,1,0:T(8,128)(2,1)}) %reduce-scatter.5.cloned.1.call-update) | async-done | bytes 2359312 | tf_op jit(solution)/shard_map/reduce_scatter | solution.py:94
  1458.2 4.5 multiply_bitcast_fusion
  1462.6 35.7 %reduce-scatter.3.cloned.1.call-done = bf16[1,128,3072]{2,1,0:T(8,128)(2,1)} async-done(((bf16[4,128,3072]{2,1,0:T(8,128)(2,1)}), bf16[1,128,3072]{2,1,0:T(8,128)(2,1)}) %reduce-scatter.3.cloned.1.call-update) | async-done | bytes 786448 | tf_op jit(solution)/shard_map/reduce_scatter | solution.py:86
  (459 shorter events, 422.0 us)
Async XLA Ops:
  7.2 264.6 %copy-start = (s32[96,12]{0,1:T(8,128)S(1)}, s32[96,12]{0,1:T(8,128)}, u32[]{:S(2)}) copy-start(s32[96,12]{0,1:T(8,128)} %param.10) | copy-start | bytes 13828
  7.2 322.6 %all-gather.2.cloned.1.call-start = ((), (), s32[]{:S(2)}) async-start(), calls=%async_computation.2 | async-start | bytes 3932160 | tf_op jit(solution)/shard_map/all_gather | solution.py:60
  7.2 57.5 %collective-permute-start = (bf16[72,128,128]{2,1,0:T(8,128)(2,1)}, bf16[72,128,128]{2,1,0:T(8,128)(2,1)S(1)}, u32[]{:S(2)}, u32[]{:S(2)}) collective-permute-start(bf16[72,128,128]{2,1,0:T(8,128)(2,1)} %bitcast.130), channel_id=1, source_target_pairs={{0,1},{1,2},{2,3},{3,4},{4,5},{5,6},{6,7},{7,0},{8,9},{9,10},{10,1... | collective-permute-start | bytes 7077896 | tf_op jit(solution)/shard_map/ppermute | solution.py:21
  64.7 100.8 %collective-permute-start.1 = (bf16[72,128,128]{2,1,0:T(8,128)(2,1)S(1)}, bf16[72,128,128]{2,1,0:T(8,128)(2,1)}, u32[]{:S(2)}, u32[]{:S(2)}) collective-permute-start(bf16[72,128,128]{2,1,0:T(8,128)(2,1)S(1)} %collective-permute-done), channel_id=1, source_target_pairs={{0,1},{1,2},{2,3},{3,4},{4,5},{5,6},{6,7},{7,0},{8,9},{9,10},{10,1... | collective-permute-start | bytes 7077896 | tf_op jit(solution)/shard_map/ppermute | solution.py:21
  64.7 103.4 %collective-permute-start.4 = (bf16[72,128,128]{2,1,0:T(8,128)(2,1)}, bf16[72,128,128]{2,1,0:T(8,128)(2,1)}, u32[]{:S(2)}, u32[]{:S(2)}) collective-permute-start(bf16[72,128,128]{2,1,0:T(8,128)(2,1)} %bitcast.131), channel_id=1, source_target_pairs={{1,0},{2,1},{3,2},{4,3},{5,4},{6,5},{7,6},{0,7},{9,8},{10,9},{11,1... | collective-permute-start | bytes 7077896 | tf_op jit(solution)/shard_map/ppermute | solution.py:23
  69.5 1388.7 %reduce-scatter.5.cloned.1.call-start = ((), (), s32[]{:S(2)}) async-start(), calls=%async_computation.4 | async-start | bytes 21233664 | tf_op jit(solution)/shard_map/reduce_scatter | solution.py:94
  165.5 102.8 %collective-permute-start.2 = (bf16[72,128,128]{2,1,0:T(8,128)(2,1)}, bf16[72,128,128]{2,1,0:T(8,128)(2,1)}, u32[]{:S(2)}, u32[]{:S(2)}) collective-permute-start(bf16[72,128,128]{2,1,0:T(8,128)(2,1)} %collective-permute-done.1), channel_id=1, source_target_pairs={{0,1},{1,2},{2,3},{3,4},{4,5},{5,6},{6,7},{7,0},{8,9},{9,10},{10,1... | collective-permute-start | bytes 7077896 | tf_op jit(solution)/shard_map/ppermute | solution.py:21
  168.1 103.8 %collective-permute-start.5 = (bf16[72,128,128]{2,1,0:T(8,128)(2,1)}, bf16[72,128,128]{2,1,0:T(8,128)(2,1)}, u32[]{:S(2)}, u32[]{:S(2)}) collective-permute-start(bf16[72,128,128]{2,1,0:T(8,128)(2,1)} %collective-permute-done.4), channel_id=1, source_target_pairs={{1,0},{2,1},{3,2},{4,3},{5,4},{6,5},{7,6},{0,7},{9,8},{10,9},{11,1... | collective-permute-start | bytes 7077896 | tf_op jit(solution)/shard_map/ppermute | solution.py:23
  268.3 102.9 %collective-permute-start.3 = (bf16[72,128,128]{2,1,0:T(8,128)(2,1)}, bf16[72,128,128]{2,1,0:T(8,128)(2,1)}, u32[]{:S(2)}, u32[]{:S(2)}) collective-permute-start(bf16[72,128,128]{2,1,0:T(8,128)(2,1)} %collective-permute-done.2), channel_id=1, source_target_pairs={{0,1},{1,2},{2,3},{3,4},{4,5},{5,6},{6,7},{7,0},{8,9},{9,10},{10,1... | collective-permute-start | bytes 7077896 | tf_op jit(solution)/shard_map/ppermute | solution.py:21
  271.9 57.9 %copy-start.6 = (s32[288]{0:T(512)}, s32[288]{0:T(512)S(1)}, u32[]{:S(2)}) copy-start(s32[288]{0:T(512)S(1)} %fusion.15) | copy-start | bytes 3460
  271.9 110.4 %collective-permute-start.6 = (bf16[72,128,128]{2,1,0:T(8,128)(2,1)}, bf16[72,128,128]{2,1,0:T(8,128)(2,1)}, u32[]{:S(2)}, u32[]{:S(2)}) collective-permute-start(bf16[72,128,128]{2,1,0:T(8,128)(2,1)} %collective-permute-done.5), channel_id=1, source_target_pairs={{1,0},{2,1},{3,2},{4,3},{5,4},{6,5},{7,6},{0,7},{9,8},{10,9},{11,1... | collective-permute-start | bytes 7077896 | tf_op jit(solution)/shard_map/ppermute | solution.py:23
  375.2 2.6 copy-start.5
  384.4 6.5 copy-start.4
  470.2 0.7 copy-start.2
  472.4 8.0 copy-start.3
  495.2 0.7 copy-start.2
  497.3 8.0 copy-start.3
  520.3 0.7 copy-start.2
  522.4 8.0 copy-start.3
  545.3 0.7 copy-start.2
  547.5 8.0 copy-start.3
  570.4 0.7 copy-start.2
  572.5 8.0 copy-start.3
  595.4 0.7 copy-start.2
  597.6 8.0 copy-start.3
  620.5 0.7 copy-start.2
  622.6 8.0 copy-start.3
  645.5 0.7 copy-start.2
  647.7 8.0 copy-start.3
  670.6 0.7 copy-start.2
  672.8 8.1 copy-start.3
  695.7 0.7 copy-start.2
  697.9 8.0 copy-start.3
  720.8 0.7 copy-start.2
  723.0 8.0 copy-start.3
  745.8 0.7 copy-start.2
  748.0 8.0 copy-start.3
  770.8 0.7 copy-start.2
  773.0 8.1 copy-start.3
  796.0 0.7 copy-start.2
  798.2 8.0 copy-start.3
  821.0 0.7 copy-start.2
  823.2 8.0 copy-start.3
  846.1 0.7 copy-start.2
  848.3 8.1 copy-start.3
  871.3 0.7 copy-start.2
  873.4 8.1 copy-start.3
  896.4 0.7 copy-start.2
  898.6 8.1 copy-start.3
  921.6 0.7 copy-start.2
  923.8 8.0 copy-start.3
  946.7 0.7 copy-start.2
  948.9 8.0 copy-start.3
  971.7 0.7 copy-start.2
  973.9 8.0 copy-start.3
  996.8 0.7 copy-start.2
  999.0 8.0 copy-start.3
  1021.9 0.7 copy-start.2
  1024.1 8.0 copy-start.3
  1047.0 0.7 copy-start.2
  1049.1 8.1 copy-start.3
  1060.2 12.6 copy-start.7
  1146.0 352.4 %reduce-scatter.3.cloned.1.call-start = ((), (), s32[]{:S(2)}) async-start(), calls=%async_computation.3 | async-start | bytes 3932160 | tf_op jit(solution)/shard_map/reduce_scatter | solution.py:86
  1158.5 339.9 %copy-start.1 = (s32[96,12]{0,1:T(8,128)S(1)}, s32[96,12]{0,1:T(8,128)}, u32[]{:S(2)}) copy-start(s32[96,12]{0,1:T(8,128)} %param.10) | copy-start | bytes 13828
Sparse Core Ops, SparseCore 0:
  69.6 25.8 all-gather.1
  1146.2 311.9 reduce-scatter.4
  1461.3 37.0 reduce-scatter.2
